TPU v7x, 256 devices: a whole 4x4x8 slice. The times are simulated.
256 devices in a mesh: sec: 4 (over z_lo), row: 8 (over y, core), rad: 8 (over z_hi, x).
Axes of the slice: x: 4, y: 4, z: 8 (z_hi: 2, z_lo: 4; z = z_hi * 4 + z_lo), core: 2. Of those that a mesh axis runs over, the one named last changes fastest.
Arguments:
- state: float32 [5, 4, 16, 64, 1024], P(None, 'sec', None, 'rad', 'row'), may hold values from -6 to 6
- volume: float32 [4, 16, 64, 1024], P('sec', None, 'rad', 'row'), may hold values from 0.5 to 2
- face_axial: float32 [4, 16, 64, 1024], P('sec', None, 'rad', 'row'), may hold values from 0.5 to 1.5
- face_radial: float32 [4, 16, 64, 1024], P('sec', None, 'rad', 'row'), may hold values from 0.5 to 1.5
- face_circum: float32 [4, 16, 64, 1024], P('sec', None, 'rad', 'row'), may hold values from 0.5 to 1.5
- viscosity: float32 [4, 16, 64, 1024], P('sec', None, 'rad', 'row'), may hold values from 0.05 to 0.5
- flux_matrix: float32 [4, 3, 5, 5], P('sec'), may hold values from -2.5 to 2.5
- inflow_plane: float32 [5, 64, 1024], P(None, 'rad', 'row'), may hold values from -6 to 6
- outflow_plane: float32 [5, 64, 1024], P(None, 'rad', 'row'), may hold values from -6 to 6
- down_donors: int32 [4, 512], P('sec', ('row', 'rad')), may hold values from 0 to 511, each once within a row
- up_donors: int32 [4, 512], P('sec', ('row', 'rad')), may hold values from 0 to 511, each once within a row
- pressure_weight: float32 [5], replicated, may hold values from -3 to 3
- boundary_coupling: float32 [5], replicated, may hold values from -4 to 4
Outputs:
- advanced: float32 [5, 4, 16, 64, 1024], P(None, 'sec', None, 'rad', 'row')
Inputs may be any that keep to these rules, and one draw needn't show every extreme that they name: `down_donors`: each row names each of the 512 tiles exactly once. `up_donors`: each row names each of the 512 tiles exactly once.
All inputs are finite; a program needn't handle non-finite values.
Results may differ from a plain program's by a relative error of at most 0.0001.
Values sent between devices are 32-bit elements; how exact they have to be, the bound alone decides.
No kernel may reach another device: no remote copies, remote signals or barrier semaphores. Data moves between devices by JAX's collectives and lax.ppermute only.
A program may use at most 64 MiB of HBM per device.

v0:
```python
import functools

import jax
import jax.numpy as jnp
from jax import lax
from jax.experimental import pallas as pl
from jax.experimental.pallas import tpu as pltpu
from jax.sharding import PartitionSpec as P


STEPS = 4
time_step = 0.08
INTERPRET = False
VMEM_LIMIT = 8 * 1024 * 1024
FAR_LIMIT = 60 * 1024 * 1024

NV = 5
ROWS = 8
FIELD_ROWS = 80
PLANES = 16
TILE_ROWS = 48


def vmem():
    return pl.BlockSpec(memory_space=pltpu.VMEM)


def smem():
    return pl.BlockSpec(memory_space=pltpu.SMEM)


def hbm():
    return pl.BlockSpec(memory_space=pltpu.HBM)


def call(kernel, outs, scalars, arrays, flops=0, scratch=(), far=()):
    moved = sum(a.size * 4 for a in arrays) + sum(4 * functools.reduce(lambda x, y: x * y, o) for o in outs)
    scratch = list(scratch)
    if far:
        scratch += [pltpu.VMEM(a.shape, jnp.float32) for a in far] + [pltpu.SemaphoreType.DMA((len(far),))]
    return pl.pallas_call(
        kernel,
        out_shape=[jax.ShapeDtypeStruct(o, jnp.float32) for o in outs],
        in_specs=[smem() for _ in scalars] + [vmem() for _ in arrays] + [hbm() for _ in far],
        out_specs=[vmem() for _ in outs],
        scratch_shapes=scratch,
        compiler_params=pltpu.CompilerParams(vmem_limit_bytes=FAR_LIMIT if far else VMEM_LIMIT),
        cost_estimate=pl.CostEstimate(flops=flops, bytes_accessed=moved, transcendentals=0),
        interpret=INTERPRET,
    )(*scalars, *arrays, *far)


def lanes_of(shape):
    return lax.broadcasted_iota(jnp.int32, shape, 1)


def rows_of(shape):
    return lax.broadcasted_iota(jnp.int32, shape, 0)


def roll(x, by, axis):
    size = x.shape[axis]
    if not isinstance(by, int):
        return pltpu.roll(x, lax.rem(by + 2 * size, size), axis)
    by %= size
    return x if by == 0 else pltpu.roll(x, by, axis)


def pressure(weight_ref, values):
    total = weight_ref[0] * values[0]
    for v in range(1, NV):
        total = total + weight_ref[v] * values[v]
    return total


def fetch(sources, targets, sems):
    copies = [pltpu.make_async_copy(a, b, sems.at[i]) for i, (a, b) in enumerate(zip(sources, targets))]
    for copy in copies:
        copy.start()
    for copy in copies:
        copy.wait()


def beside_kernel(weight, state_hbm, beside, inlet, sem):
    copies = [
        pltpu.make_async_copy(state_hbm.at[:, PLANES - 1], beside.at[pl.ds(0, NV)], sem.at[0]),
        pltpu.make_async_copy(state_hbm.at[:, 0], inlet, sem.at[1]),
    ]
    for copy in copies:
        copy.start()
    for copy in copies:
        copy.wait()
    beside[NV] = pressure(weight, [inlet[v] for v in range(NV)])


def first_kernel(ids, weight, down_donors, up_donors, *refs):
    sources, (out_pressure, send, first_swap, second_swap), targets, sems = refs[:5], refs[5:9], refs[9:14], refs[14]
    fetch(sources, targets, sems)
    state, radial, circ, mu, outflow = targets
    lanes = lanes_of((8, 128))
    row, size = ids[1], send.shape[0]
    out_pressure[...] = pressure(weight, [outflow[v] for v in range(NV)])
    listed = jnp.zeros((8, 128), jnp.int32)
    for a in range(8):
        listed = jnp.where(lanes == a, down_donors[a], listed)
        listed = jnp.where(lanes == 8 + a, up_donors[a], listed)
    listed = listed.astype(jnp.float32)
    for j in range(size):
        send[j, 0:8, :] = listed

    even = lax.rem(ids[2], 2) == 0

    def put(at, cell):
        first_swap[pl.ds(at, 1), :] = jnp.where(even, cell[7:8], cell[0:1])
        second_swap[pl.ds(at, 1), :] = jnp.where(even, cell[0:1], cell[7:8])

    def one(k, carry):
        last, first = carry
        for v in range(NV):
            cell = state[v, k]
            at = v * 16 + k
            put(at, cell)
            here = lanes == at
            last = jnp.where(here, roll(cell, at + 1, 1), last)
            first = jnp.where(here, roll(cell, at, 1), first)
        put(FIELD_ROWS + k, mu[k])
        put(FIELD_ROWS + 16 + k, radial[k])
        here = lanes == 80 + k
        last = jnp.where(here, roll(mu[k], 81 + k, 1), last)
        first = jnp.where(here, roll(mu[k], 80 + k, 1), first)
        last = jnp.where(lanes == 96 + k, roll(circ[k], 97 + k, 1), last)
        return last, first

    zero = jnp.zeros((8, 128), jnp.float32)
    last, first = lax.fori_loop(0, PLANES, one, (zero, zero))
    send[lax.rem(row + 1, size), 8:16, :] = last
    send[lax.rem(row + size - 1, size), 8:16, :] = first


def gather_kernel(ids, one_way, other_way, inflow, out_pressure, *refs):
    send = refs[-1]
    if len(refs) > 1:
        ends, rad = refs[0], ids[2]
        for target, row, inside in ((rad + 1, 7, rad < send.shape[0] - 1), (rad - 1, 0, rad > 0)):

            @pl.when(inside)
            def _():
                for n in range(2):
                    for v in range(NV):
                        at = TILE_ROWS + n * NV + v
                        spot = jnp.clip(target, 0, send.shape[0] - 1)
                        send[spot, at : at + 1, :] = ends[n, v, row : row + 1, :]

    section = ids[0]
    odd = lax.rem(section, 2) == 1
    size = send.shape[0]
    for v in range(NV):
        value = jnp.where(section == 0, inflow[v], jnp.where(odd, one_way[v], other_way[v]))
        for j in range(size):
            send[j, v * 8 : v * 8 + 8, :] = value
    value = jnp.where(section == ids[4] - 1, out_pressure[...], jnp.where(odd, other_way[NV], one_way[NV]))
    for j in range(size):
        send[j, 40:48, :] = value


def select_kernel(step, ids, wanted, got, *refs):
    send = refs[-1]
    size = send.shape[0]
    row = ids[1]

    def one(j, carry):
        for a in range(8):
            d = wanted[j, a] & 63
            r, b = d >> 3, d & 7
            for v in range(NV):
                send[j, v * 8 + a : v * 8 + a + 1, :] = got[r, pl.ds(v * 8 + b, 1), :]
            e = wanted[j, 8 + a] & 63
            send[j, 40 + a : 41 + a, :] = got[e >> 3, pl.ds(40 + (e & 7), 1), :]
        return carry

    lax.fori_loop(0, size, one, 0)
    if step:
        edges = refs[0]
        send[lax.rem(row + 1, size), 48:56, :] = edges[0]
        send[lax.rem(row + size - 1, size), 48:56, :] = edges[1]


def sides(step, ids, around):
    base = 48 if step else 8
    row, row_size = ids[1], ids[5]
    left = around[lax.rem(row + row_size - 1, row_size), base : base + ROWS, :]
    right = around[lax.rem(row + 1, row_size), base : base + ROWS, :]
    return left, right


def settle(ids, first_swap, second_swap, low, high):
    even = lax.rem(ids[2], 2) == 0
    low[...] = jnp.where(even, second_swap[...], first_swap[...])
    high[...] = jnp.where(even, first_swap[...], second_swap[...])


def beyond(ref, at):
    return jnp.broadcast_to(ref[pl.ds(at, 1), :], (ROWS, 128))


def coef_kernel(ids, volume, axial, radial, circ, mu, around, first_swap, second_swap, coef, low, high):
    settle(ids, first_swap, second_swap, low, high)
    rad, rad_size = ids[2], ids[3]
    lanes = lanes_of((ROWS, 128))
    rows = rows_of((ROWS, 128))
    casing = jnp.logical_and(rad == rad_size - 1, rows == 7)
    left, right = sides(0, ids, around)

    def one(k, carry):
        m = mu[k]
        c = time_step / volume[k]
        half = 0.5 * c
        diffused = []

        def put(at, area, viscous):
            coef[at, k] = half * area
            b = c * area * viscous
            coef[at + 1, k] = b
            diffused.append(b)

        lower, upper = jnp.maximum(k - 1, 0), jnp.minimum(k + 1, PLANES - 1)
        put(0, axial[lower], 0.5 * (m + mu[lower]))
        put(2, axial[k], 0.5 * (m + mu[upper]))
        face = jnp.where(casing, 0.0, radial[k])
        face_below = jnp.where(rows == 0, beyond(low, FIELD_ROWS + 16 + k), roll(face, 1, 0))
        mu_below = jnp.where(rows == 0, beyond(low, FIELD_ROWS + k), roll(m, 1, 0))
        mu_above = jnp.where(rows == 7, beyond(high, FIELD_ROWS + k), roll(m, 7, 0))
        put(4, face_below, 0.5 * (m + mu_below))
        put(6, face, 0.5 * (m + mu_above))
        ring = circ[k]
        at = 80 + k
        mu_left = jnp.where(lanes == 0, roll(left, -at, 1), roll(m, 1, 1))
        mu_right = jnp.where(lanes == 127, roll(right, 127 - at, 1), roll(m, 127, 1))
        circ_left = jnp.where(lanes == 0, roll(left, -(at + 16), 1), roll(ring, 1, 1))
        put(8, circ_left, 0.5 * (mu_left + m))
        put(10, ring, 0.5 * (m + mu_right))
        total = diffused[0]
        for b in diffused[1:]:
            total = total + b
        coef[12, k] = 1.0 - total
        return carry

    lax.fori_loop(0, PLANES, one, 0)


def advance(k, before, here, after, coef, matrix, left, right, low, high):
    lanes = lanes_of((ROWS, 128))
    rows = rows_of((ROWS, 128))
    rest = coef[12, k]
    total = [rest * here[v] for v in range(NV)]
    for d in range(3):
        low_a, low_b = coef[4 * d, k], coef[4 * d + 1, k]
        high_a, high_b = coef[4 * d + 2, k], coef[4 * d + 3, k]
        own_a = high_a - low_a
        mixed = []
        for v in range(NV):
            cell = here[v]
            at = v * 16 + k
            if d == 0:
                lower, upper = before[v], after[v]
            elif d == 1:
                lower = jnp.where(rows == 0, beyond(low, at), roll(cell, 1, 0))
                upper = jnp.where(rows == 7, beyond(high, at), roll(cell, 7, 0))
            else:
                lower = jnp.where(lanes == 0, roll(left, -at, 1), roll(cell, 1, 1))
                upper = jnp.where(lanes == 127, roll(right, 127 - at, 1), roll(cell, 127, 1))
            mixed.append(high_a * upper - low_a * lower + own_a * cell)
            total[v] = total[v] + (high_b * upper + low_b * lower)
        for u in range(NV):
            for v in range(NV):
                at = 25 * d + 5 * u + v
                total[u] = total[u] - jnp.broadcast_to(matrix[at : at + 1, :], (ROWS, 128)) * mixed[v]
    return total


def ghosts_of(ids, wanted, weight, coupling, field, across, ghost):
    for a in range(8):
        d = wanted[ids[1], a] >> 6
        for v in range(NV):
            ghost[v, a : a + 1, :] = across[d, v * 8 + a : v * 8 + a + 1, :]
        e = wanted[ids[1], 8 + a] >> 6
        ghost[NV, a : a + 1, :] = across[e, 40 + a : 41 + a, :]
    outlet = [field[v, PLANES - 1] for v in range(NV)]
    jump = ghost[NV] - pressure(weight, outlet)
    return [ghost[v] for v in range(NV)], [outlet[v] + coupling[v] * jump for v in range(NV)]


def ends_of(step, ids, wanted, weight, coupling, field, coef, matrix, across, around, low, high, ghost):
    lanes = lanes_of((ROWS, 128))
    left, right = sides(step, ids, around)
    inlet_ghost, outlet_ghost = ghosts_of(ids, wanted, weight, coupling, field, across, ghost)
    plane = lambda k: [field[v, k] for v in range(NV)]
    new_inlet = advance(0, inlet_ghost, plane(0), plane(1), coef, matrix, left, right, low, high)
    last = PLANES - 1
    new_outlet = advance(last, plane(last - 1), plane(last), outlet_ghost, coef, matrix, left, right, low, high)
    return new_inlet, new_outlet


def ends_kernel(step, ids, wanted, weight, coupling, field, coef, matrix, across, around, *refs):
    ends, beside, ghost, low, high = refs[-5:]
    if step == 0:
        settle(ids, refs[0], refs[1], low, high)
    else:
        got, rad = refs[0], ids[2]
        size = got.shape[0]
        below, above = jnp.maximum(rad - 1, 0), jnp.minimum(rad + 1, size - 1)
        for n, k in enumerate((0, PLANES - 1)):
            for v in range(NV):
                at, spot = TILE_ROWS + n * NV + v, v * 16 + k
                low[spot : spot + 1, :] = jnp.where(rad == 0, 0.0, got[below, at : at + 1, :])
                high[spot : spot + 1, :] = jnp.where(rad == size - 1, 0.0, got[above, at : at + 1, :])
    new_inlet, new_outlet = ends_of(step, ids, wanted, weight, coupling, field, coef, matrix, across, around, low, high, ghost)
    for v in range(NV):
        ends[0, v] = new_inlet[v]
        ends[1, v] = new_outlet[v]
        beside[v] = new_outlet[v]
    beside[NV] = pressure(weight, new_inlet)


def bulk_kernel(step, ids, field, coef, matrix, around, from_first, from_second, ends, new, *refs):
    low, high = refs[-2:]
    if len(refs) > 2:
        edges, first_swap, second_swap = refs[:3]
    settle(ids, from_first, from_second, low, high)
    even = lax.rem(ids[2], 2) == 0
    lanes = lanes_of((ROWS, 128))
    left, right = sides(step, ids, around)

    def note(k, total, last, first):
        for v in range(NV):
            new[v, k] = total[v]
            if len(refs) == 2:
                continue
            at = v * 16 + k
            first_swap[pl.ds(at, 1), :] = jnp.where(even, total[v][7:8], total[v][0:1])
            second_swap[pl.ds(at, 1), :] = jnp.where(even, total[v][0:1], total[v][7:8])
            spot = lanes == at
            last = jnp.where(spot, roll(total[v], at + 1, 1), last)
            first = jnp.where(spot, roll(total[v], at, 1), first)
        return last, first

    def one(k, carry):
        before, here, last, first = carry
        after = [field[v, k + 1] for v in range(NV)]
        total = advance(k, before, here, after, coef, matrix, left, right, low, high)
        last, first = note(k, total, last, first)
        return here, after, last, first

    zero = jnp.zeros((ROWS, 128), jnp.float32)
    last, first = note(0, [ends[0, v] for v in range(NV)], zero, zero)
    last, first = note(PLANES - 1, [ends[1, v] for v in range(NV)], last, first)
    carry = ([field[v, 0] for v in range(NV)], [field[v, 1] for v in range(NV)], last, first)
    _, _, last, first = lax.fori_loop(1, PLANES - 1, one, carry)
    if len(refs) > 2:
        edges[0] = last
        edges[1] = first


def body(
    state,
    volume,
    face_axial,
    face_radial,
    face_circum,
    viscosity,
    flux_matrix,
    inflow_plane,
    outflow_plane,
    down_donors,
    up_donors,
    pressure_weight,
    boundary_coupling,
):
    sections, row_size, rad_size = lax.axis_size("sec"), lax.axis_size("row"), lax.axis_size("rad")
    ids = jnp.stack(
        [
            lax.axis_index("sec"),
            lax.axis_index("row"),
            lax.axis_index("rad"),
            jnp.int32(rad_size),
            jnp.int32(sections),
            jnp.int32(row_size),
        ]
    ).astype(jnp.int32)
    own = [state[:, 0], volume[0], face_axial[0], face_radial[0], face_circum[0], viscosity[0]]
    matrix = jnp.broadcast_to(jnp.pad(flux_matrix[0].reshape(75), (0, 5))[:, None], (80, 128))
    extended = (NV, PLANES, ROWS, 128)
    strips = (2, ROWS, 128)
    sent = (FIELD_ROWS + 32, 128)
    scalars = [pressure_weight, boundary_coupling]

    beside = pl.pallas_call(
        beside_kernel,
        out_shape=jax.ShapeDtypeStruct((NV + 1, 8, 128), jnp.float32),
        in_specs=[smem(), hbm()],
        out_specs=vmem(),
        scratch_shapes=[pltpu.VMEM((NV, 8, 128), jnp.float32), pltpu.SemaphoreType.DMA((2,))],
        name="beside",
        compiler_params=pltpu.CompilerParams(vmem_limit_bytes=FAR_LIMIT),
        interpret=INTERPRET,
    )(pressure_weight, own[0])
    out_pressure, lists, first_swap, second_swap = call(
        first_kernel,
        [(8, 128), (row_size, 16, 128), sent, sent],
        [ids, pressure_weight, down_donors[0], up_donors[0]],
        [],
        far=[own[0], own[3], own[4], own[5], outflow_plane],
    )

    def swaps(size, begin):
        return [pair for i in range(begin, size - 1, 2) for pair in ((i, i + 1), (i + 1, i))]

    table = lax.all_to_all(lists, "row", 0, 0)
    wanted = table[:, 0, :16].astype(jnp.int32)
    field = own[0]
    coef = edges = None
    for step in range(STEPS):
        last_step = step == STEPS - 1
        one_way = lax.ppermute(beside, "sec", swaps(sections, 0))
        other_way = lax.ppermute(beside, "sec", swaps(sections, 1))
        (send,) = call(
            gather_kernel,
            [(rad_size, TILE_ROWS + (16 if step else 0), 128)],
            [ids],
            [one_way, other_way, inflow_plane, out_pressure] + ([ends] if step else []),
        )
        got = lax.all_to_all(send, "rad", 0, 0)
        high = lax.ppermute(second_swap, "rad", swaps(rad_size, 1))
        low = lax.ppermute(first_swap, "rad", swaps(rad_size, 0))
        strip = [pltpu.VMEM(low.shape, jnp.float32)] * 2
        if step == 0:
            (coef,) = call(coef_kernel, [(13, PLANES, ROWS, 128)], [ids], own[1:] + [table, low, high], scratch=strip)
        (send,) = call(
            functools.partial(select_kernel, step),
            [(row_size, TILE_ROWS + (ROWS if step else 0), 128)],
            [ids, wanted],
            [got, edges] if step else [got],
        )
        across = lax.all_to_all(send, "row", 0, 0)
        around = across if step else table
        ghost = [pltpu.VMEM((NV + 1, ROWS, 128), jnp.float32)]
        ends, beside = call(
            functools.partial(ends_kernel, step),
            [(2, NV, ROWS, 128), (NV + 1, 8, 128)],
            [ids, wanted] + scalars,
            [field, coef, matrix, across, around] + ([got] if step else [low, high]),
            flops=2 * ROWS * 128 * 300,
            scratch=ghost + strip,
        )
        result = call(
            functools.partial(bulk_kernel, step),
            [extended] + ([] if last_step else [strips, (FIELD_ROWS, 128), (FIELD_ROWS, 128)]),
            [ids],
            [field, coef, matrix, around, low, high, ends],
            flops=PLANES * ROWS * 128 * 300,
            scratch=strip,
        )
        field = result[0]
        if not last_step:
            edges, first_swap, second_swap = result[1:]
    return field[:, None]


def solution(mesh):
    in_specs = (
        P(None, "sec", None, "rad", "row"),
        P("sec", None, "rad", "row"),
        P("sec", None, "rad", "row"),
        P("sec", None, "rad", "row"),
        P("sec", None, "rad", "row"),
        P("sec", None, "rad", "row"),
        P("sec", None, None, None),
        P(None, "rad", "row"),
        P(None, "rad", "row"),
        P("sec", ("row", "rad")),
        P("sec", ("row", "rad")),
        P(),
        P(),
    )
    out_specs = P(None, "sec", None, "rad", "row")

    return jax.shard_map(body, mesh=mesh, in_specs=in_specs, out_specs=out_specs, check_vma=False)
```

profile of v0, /device:TPU:46, one launch (start us, length us, event | category | flops | bytes accessed | tf_op | source)
XLA Modules:
  0.0 192.0 jit_solution(7482848805441156866)
XLA Ops:
  0.7 3.9 %shard_map.127 = (f32[8,128]{1,0:T(8,128)}, f32[8,16,128]{2,1,0:T(8,128)}, f32[112,128]{1,0:T(8,128)}, f32[112,128]{1,0:T(8,128)}) custom-call(s32[6]{0:T(128)} %stack.15.ids, f32[5]{0:T(128)} %weight.11, s32[8]{0:T(128)} %bitcast.35, s32[8]{0:T(128)} %bitcast.36, f32[5,16,8,128]{3,2,1,0:T(8,128)} %bitcast.15, f32[16,8,128]{2,1,0:T(8,128)} %bitcast.27, ...), custom_call_target="tpu_custom_call" | custom-call | bytes 184320 | tf_op jit(solution)/shard_map/pallas_call | solution.py:41
  4.6 4.9 %all-to-all-start = ((f32[8,16,128]{2,1,0:T(8,128)}), f32[8,16,128]{2,1,0:T(8,128)S(1)}, u32[]{:S(2)}, u32[]{:S(2)}) async-start(f32[8,16,128]{2,1,0:T(8,128)} %get-tuple-element.28), calls=%async_computation | async-start | bytes 131072 | tf_op jit(solution)/shard_map/all_to_all | solution.py:418
  11.7 3.8 %collective-permute-start.3 = (f32[6,8,128]{2,1,0:T(8,128)}, f32[6,8,128]{2,1,0:T(8,128)S(1)}, u32[]{:S(2)}, u32[]{:S(2)}) collective-permute-start(f32[6,8,128]{2,1,0:T(8,128)} %beside.1), channel_id=1, source_target_pairs={{64,128},{128,64},{65,129},{129,65},{66,130},{130,66},{67,131},{13... | collective-permute-start | bytes 73736 | tf_op jit(solution)/shard_map/ppermute | solution.py:425
  20.9 9.6 %all-to-all-start.1 = ((f32[8,48,128]{2,1,0:T(8,128)}), f32[8,48,128]{2,1,0:T(8,128)S(1)}, u32[]{:S(2)}, u32[]{:S(2)}) async-start(f32[8,48,128]{2,1,0:T(8,128)} %shard_map.129), calls=%async_computation.1 | async-start | bytes 393216 | tf_op jit(solution)/shard_map/all_to_all | solution.py:432
  30.5 9.5 %all-to-all-done.1.got = f32[8,48,128]{2,1,0:T(8,128)S(1)} async-done(((f32[8,48,128]{2,1,0:T(8,128)}), f32[8,48,128]{2,1,0:T(8,128)S(1)}, u32[]{:S(2)}, u32[]{:S(2)}) %all-to-all-start.1) | async-done | bytes 196640 | tf_op jit(solution)/shard_map/all_to_all | solution.py:432
  41.7 4.9 %all-to-all-start.2 = ((f32[8,48,128]{2,1,0:T(8,128)}), f32[8,48,128]{2,1,0:T(8,128)S(1)}, u32[]{:S(2)}, u32[]{:S(2)}) async-start(f32[8,48,128]{2,1,0:T(8,128)} %shard_map.130), calls=%async_computation.2 | async-start | bytes 393216 | tf_op jit(solution)/shard_map/all_to_all | solution.py:444
  47.2 4.0 %collective-permute-start.1 = (f32[112,128]{1,0:T(8,128)S(1)}, f32[112,128]{1,0:T(8,128)S(1)}, u32[]{:S(2)}, u32[]{:S(2)}) collective-permute-start(f32[112,128]{1,0:T(8,128)S(1)} %copy-done.12), channel_id=1, source_target_pairs={{1,2},{2,1},{3,4},{4,3},{5,6},{6,5},{9,10},{10,9},{11,12},{12,11},... | collective-permute-start | bytes 172040 | tf_op jit(solution)/shard_map/ppermute | solution.py:433
  51.4 8.0 %collective-permute-done.1.second_swap.refs_1_.from_second = f32[112,128]{1,0:T(8,128)S(1)} collective-permute-done((f32[112,128]{1,0:T(8,128)S(1)}, f32[112,128]{1,0:T(8,128)S(1)}, u32[]{:S(2)}, u32[]{:S(2)}) %collective-permute-start.1) | collective-permute-done | bytes 57376 | tf_op jit(solution)/shard_map/ppermute | solution.py:433
  70.8 4.5 %all-to-all-start.3 = ((f32[8,64,128]{2,1,0:T(8,128)}), f32[8,64,128]{2,1,0:T(8,128)S(1)}, u32[]{:S(2)}, u32[]{:S(2)}) async-start(f32[8,64,128]{2,1,0:T(8,128)} %shard_map.133), calls=%async_computation.3 | async-start | bytes 524288 | tf_op jit(solution)/shard_map/all_to_all | solution.py:432
  75.3 3.1 %shard_map.132 = (f32[5,16,8,128]{3,2,1,0:T(8,128)S(1)}, f32[2,8,128]{2,1,0:T(8,128)S(1)}, f32[80,128]{1,0:T(8,128)S(1)}, f32[80,128]{1,0:T(8,128)S(1)}) custom-call(s32[6]{0:T(128)S(1)} %copy-done.5, f32[5,16,8,128]{3,2,1,0:T(8,128)S(1)} %bitcast.18, f32[13,16,8,128]{3,2,1,0:T(8,128)S(1)} %shard_map.128.coef, f32[80,128]{1,0:T(8,128)S(1)} %broadcast_in_dim.4.matrix, ...), custom_call_target="tpu_custom_call" | custom-call | flops 4915200 | bytes 1859584 | tf_op jit(solution)/shard_map/pallas_call | solution.py:41
  78.4 6.9 %all-to-all-done.3.got.refs_0_ = f32[8,64,128]{2,1,0:T(8,128)S(1)} async-done(((f32[8,64,128]{2,1,0:T(8,128)}), f32[8,64,128]{2,1,0:T(8,128)S(1)}, u32[]{:S(2)}, u32[]{:S(2)}) %all-to-all-start.3) | async-done | bytes 262176 | tf_op jit(solution)/shard_map/all_to_all | solution.py:432
  86.3 10.3 %all_to_all.45.across.around = f32[8,56,128]{2,1,0:T(8,128)S(1)} all-to-all(f32[8,56,128]{2,1,0:T(8,128)S(1)} %shard_map.134), channel_id=1, replica_groups=mesh['sec'=4,'row'=8,'rad'=8] {'row'}, dimensions={0} | all-to-all | bytes 458752 | tf_op jit(solution)/shard_map/all_to_all | solution.py:444
  105.5 5.7 %all-to-all-start.5 = ((f32[8,64,128]{2,1,0:T(8,128)}), f32[8,64,128]{2,1,0:T(8,128)S(1)}, u32[]{:S(2)}, u32[]{:S(2)}) async-start(f32[8,64,128]{2,1,0:T(8,128)} %shard_map.137), calls=%async_computation.5 | async-start | bytes 524288 | tf_op jit(solution)/shard_map/all_to_all | solution.py:432
  112.1 7.9 %collective-permute-start.7 = (f32[80,128]{1,0:T(8,128)S(1)}, f32[80,128]{1,0:T(8,128)S(1)}, u32[]{:S(2)}, u32[]{:S(2)}) collective-permute-start(f32[80,128]{1,0:T(8,128)S(1)} %get-tuple-element.37), channel_id=1, source_target_pairs={{1,2},{2,1},{3,4},{4,3},{5,6},{6,5},{9,10},{10,9},{11,12},{12,11},... | collective-permute-start | bytes 122888 | tf_op jit(solution)/shard_map/ppermute | solution.py:433
  120.0 4.3 %collective-permute-done.7.from_second = f32[80,128]{1,0:T(8,128)S(1)} collective-permute-done((f32[80,128]{1,0:T(8,128)S(1)}, f32[80,128]{1,0:T(8,128)S(1)}, u32[]{:S(2)}, u32[]{:S(2)}) %collective-permute-start.7) | collective-permute-done | bytes 40992 | tf_op jit(solution)/shard_map/ppermute | solution.py:433
  124.3 3.1 %shard_map.136 = (f32[5,16,8,128]{3,2,1,0:T(8,128)S(1)}, f32[2,8,128]{2,1,0:T(8,128)S(1)}, f32[80,128]{1,0:T(8,128)S(1)}, f32[80,128]{1,0:T(8,128)S(1)}) custom-call(s32[6]{0:T(128)S(1)} %copy-done.5, f32[5,16,8,128]{3,2,1,0:T(8,128)S(1)} %get-tuple-element.33.field, f32[13,16,8,128]{3,2,1,0:T(8,128)S(1)} %shard_map.128.coef, ...), custom_call_target="tpu_custom_call" | custom-call | flops 4915200 | bytes 1990656 | tf_op jit(solution)/shard_map/pallas_call | solution.py:41
  128.4 9.6 %all_to_all.46.across.around = f32[8,56,128]{2,1,0:T(8,128)S(1)} all-to-all(f32[8,56,128]{2,1,0:T(8,128)S(1)} %shard_map.138), channel_id=1, replica_groups=mesh['sec'=4,'row'=8,'rad'=8] {'row'}, dimensions={0} | all-to-all | bytes 458752 | tf_op jit(solution)/shard_map/all_to_all | solution.py:444
  138.7 2.9 %collective-permute-start.13 = (f32[6,8,128]{2,1,0:T(8,128)S(1)}, f32[6,8,128]{2,1,0:T(8,128)S(1)}, u32[]{:S(2)}, u32[]{:S(2)}) collective-permute-start(f32[6,8,128]{2,1,0:T(8,128)S(1)} %get-tuple-element.46), channel_id=1, source_target_pairs={{64,128},{128,64},{65,129},{129,65},{66,130},{130,66},{67,131},{13... | collective-permute-start | bytes 73736 | tf_op jit(solution)/shard_map/ppermute | solution.py:425
  146.9 7.8 %all-to-all-start.7 = ((f32[8,64,128]{2,1,0:T(8,128)}), f32[8,64,128]{2,1,0:T(8,128)S(1)}, u32[]{:S(2)}, u32[]{:S(2)}) async-start(f32[8,64,128]{2,1,0:T(8,128)} %shard_map.141), calls=%async_computation.7 | async-start | bytes 524288 | tf_op jit(solution)/shard_map/all_to_all | solution.py:432
  155.6 7.9 %collective-permute-start.11 = (f32[80,128]{1,0:T(8,128)S(1)}, f32[80,128]{1,0:T(8,128)S(1)}, u32[]{:S(2)}, u32[]{:S(2)}) collective-permute-start(f32[80,128]{1,0:T(8,128)S(1)} %get-tuple-element.43), channel_id=1, source_target_pairs={{1,2},{2,1},{3,4},{4,3},{5,6},{6,5},{9,10},{10,9},{11,12},{12,11},... | collective-permute-start | bytes 122888 | tf_op jit(solution)/shard_map/ppermute | solution.py:433
  163.5 4.3 %collective-permute-done.11.from_second = f32[80,128]{1,0:T(8,128)S(1)} collective-permute-done((f32[80,128]{1,0:T(8,128)S(1)}, f32[80,128]{1,0:T(8,128)S(1)}, u32[]{:S(2)}, u32[]{:S(2)}) %collective-permute-start.11) | collective-permute-done | bytes 40992 | tf_op jit(solution)/shard_map/ppermute | solution.py:433
  167.8 3.1 %shard_map.140 = (f32[5,16,8,128]{3,2,1,0:T(8,128)S(1)}, f32[2,8,128]{2,1,0:T(8,128)S(1)}, f32[80,128]{1,0:T(8,128)S(1)}, f32[80,128]{1,0:T(8,128)S(1)}) custom-call(s32[6]{0:T(128)S(1)} %copy-done.5, f32[5,16,8,128]{3,2,1,0:T(8,128)S(1)} %get-tuple-element.39.field, f32[13,16,8,128]{3,2,1,0:T(8,128)S(1)} %shard_map.128.coef, ...), custom_call_target="tpu_custom_call" | custom-call | flops 4915200 | bytes 1990656 | tf_op jit(solution)/shard_map/pallas_call | solution.py:41
  172.5 4.8 %all-to-all-start.8 = ((f32[8,56,128]{2,1,0:T(8,128)}), f32[8,56,128]{2,1,0:T(8,128)S(1)}, u32[]{:S(2)}, u32[]{:S(2)}) async-start(f32[8,56,128]{2,1,0:T(8,128)} %shard_map.142), calls=%async_computation.8 | async-start | bytes 458752 | tf_op jit(solution)/shard_map/all_to_all | solution.py:444
  177.3 7.9 %collective-permute-start.15 = (f32[80,128]{1,0:T(8,128)S(1)}, f32[80,128]{1,0:T(8,128)S(1)}, u32[]{:S(2)}, u32[]{:S(2)}) collective-permute-start(f32[80,128]{1,0:T(8,128)S(1)} %get-tuple-element.49), channel_id=1, source_target_pairs={{1,2},{2,1},{3,4},{4,3},{5,6},{6,5},{9,10},{10,9},{11,12},{12,11},... | collective-permute-start | bytes 122888 | tf_op jit(solution)/shard_map/ppermute | solution.py:433
  (77 shorter events, 48.9 us)
Async XLA Ops:
  4.6 16.3 %all-to-all-start = ((f32[8,16,128]{2,1,0:T(8,128)}), f32[8,16,128]{2,1,0:T(8,128)S(1)}, u32[]{:S(2)}, u32[]{:S(2)}) async-start(f32[8,16,128]{2,1,0:T(8,128)} %get-tuple-element.28), calls=%async_computation | async-start | bytes 131072 | tf_op jit(solution)/shard_map/all_to_all | solution.py:418
  11.7 5.9 %collective-permute-start.3 = (f32[6,8,128]{2,1,0:T(8,128)}, f32[6,8,128]{2,1,0:T(8,128)S(1)}, u32[]{:S(2)}, u32[]{:S(2)}) collective-permute-start(f32[6,8,128]{2,1,0:T(8,128)} %beside.1), channel_id=1, source_target_pairs={{64,128},{128,64},{65,129},{129,65},{66,130},{130,66},{67,131},{13... | collective-permute-start | bytes 73736 | tf_op jit(solution)/shard_map/ppermute | solution.py:425
  15.6 4.1 %collective-permute-start.2 = (f32[6,8,128]{2,1,0:T(8,128)}, f32[6,8,128]{2,1,0:T(8,128)S(1)}, u32[]{:S(2)}, u32[]{:S(2)}) collective-permute-start(f32[6,8,128]{2,1,0:T(8,128)} %beside.1), channel_id=1, source_target_pairs={{0,64},{64,0},{128,192},{192,128},{1,65},{65,1},{129,193},{193,129... | collective-permute-start | bytes 73736 | tf_op jit(solution)/shard_map/ppermute | solution.py:424
  20.9 19.1 %all-to-all-start.1 = ((f32[8,48,128]{2,1,0:T(8,128)}), f32[8,48,128]{2,1,0:T(8,128)S(1)}, u32[]{:S(2)}, u32[]{:S(2)}) async-start(f32[8,48,128]{2,1,0:T(8,128)} %shard_map.129), calls=%async_computation.1 | async-start | bytes 393216 | tf_op jit(solution)/shard_map/all_to_all | solution.py:432
  41.7 17.7 %copy-start.3 = (f32[1,16,8,128]{3,2,1,0:T(8,128)S(1)}, f32[1,16,8,128]{3,2,1,0:T(8,128)}, u32[]{:S(2)}) copy-start(f32[1,16,8,128]{3,2,1,0:T(8,128)} %param.17) | copy-start | bytes 196612
  41.7 19.5 %all-to-all-start.2 = ((f32[8,48,128]{2,1,0:T(8,128)}), f32[8,48,128]{2,1,0:T(8,128)S(1)}, u32[]{:S(2)}, u32[]{:S(2)}) async-start(f32[8,48,128]{2,1,0:T(8,128)} %shard_map.130), calls=%async_computation.2 | async-start | bytes 393216 | tf_op jit(solution)/shard_map/all_to_all | solution.py:444
  46.7 4.7 %collective-permute-start = (f32[112,128]{1,0:T(8,128)S(1)}, f32[112,128]{1,0:T(8,128)S(1)}, u32[]{:S(2)}, u32[]{:S(2)}) collective-permute-start(f32[112,128]{1,0:T(8,128)S(1)} %copy-done.13), channel_id=1, source_target_pairs={{0,1},{1,0},{2,3},{3,2},{4,5},{5,4},{6,7},{7,6},{8,9},{9,8},{10,11... | collective-permute-start | bytes 172040 | tf_op jit(solution)/shard_map/ppermute | solution.py:434
  47.2 12.2 %collective-permute-start.1 = (f32[112,128]{1,0:T(8,128)S(1)}, f32[112,128]{1,0:T(8,128)S(1)}, u32[]{:S(2)}, u32[]{:S(2)}) collective-permute-start(f32[112,128]{1,0:T(8,128)S(1)} %copy-done.12), channel_id=1, source_target_pairs={{1,2},{2,1},{3,4},{4,3},{5,6},{6,5},{9,10},{10,9},{11,12},{12,11},... | collective-permute-start | bytes 172040 | tf_op jit(solution)/shard_map/ppermute | solution.py:433
  62.7 5.7 %collective-permute-start.5 = (f32[6,8,128]{2,1,0:T(8,128)S(1)}, f32[6,8,128]{2,1,0:T(8,128)S(1)}, u32[]{:S(2)}, u32[]{:S(2)}) collective-permute-start(f32[6,8,128]{2,1,0:T(8,128)S(1)} %get-tuple-element.34), channel_id=1, source_target_pairs={{64,128},{128,64},{65,129},{129,65},{66,130},{130,66},{67,131},{13... | collective-permute-start | bytes 73736 | tf_op jit(solution)/shard_map/ppermute | solution.py:425
  65.6 3.9 %collective-permute-start.4 = (f32[6,8,128]{2,1,0:T(8,128)S(1)}, f32[6,8,128]{2,1,0:T(8,128)S(1)}, u32[]{:S(2)}, u32[]{:S(2)}) collective-permute-start(f32[6,8,128]{2,1,0:T(8,128)S(1)} %get-tuple-element.34), channel_id=1, source_target_pairs={{0,64},{64,0},{128,192},{192,128},{1,65},{65,1},{129,193},{193,129... | collective-permute-start | bytes 73736 | tf_op jit(solution)/shard_map/ppermute | solution.py:424
  70.8 14.5 %all-to-all-start.3 = ((f32[8,64,128]{2,1,0:T(8,128)}), f32[8,64,128]{2,1,0:T(8,128)S(1)}, u32[]{:S(2)}, u32[]{:S(2)}) async-start(f32[8,64,128]{2,1,0:T(8,128)} %shard_map.133), calls=%async_computation.3 | async-start | bytes 524288 | tf_op jit(solution)/shard_map/all_to_all | solution.py:432
  97.4 5.7 %collective-permute-start.9 = (f32[6,8,128]{2,1,0:T(8,128)S(1)}, f32[6,8,128]{2,1,0:T(8,128)S(1)}, u32[]{:S(2)}, u32[]{:S(2)}) collective-permute-start(f32[6,8,128]{2,1,0:T(8,128)S(1)} %get-tuple-element.40), channel_id=1, source_target_pairs={{64,128},{128,64},{65,129},{129,65},{66,130},{130,66},{67,131},{13... | collective-permute-start | bytes 73736 | tf_op jit(solution)/shard_map/ppermute | solution.py:425
  100.3 3.9 %collective-permute-start.8 = (f32[6,8,128]{2,1,0:T(8,128)S(1)}, f32[6,8,128]{2,1,0:T(8,128)S(1)}, u32[]{:S(2)}, u32[]{:S(2)}) collective-permute-start(f32[6,8,128]{2,1,0:T(8,128)S(1)} %get-tuple-element.40), channel_id=1, source_target_pairs={{0,64},{64,0},{128,192},{192,128},{1,65},{65,1},{129,193},{193,129... | collective-permute-start | bytes 73736 | tf_op jit(solution)/shard_map/ppermute | solution.py:424
  105.5 21.9 %all-to-all-start.5 = ((f32[8,64,128]{2,1,0:T(8,128)}), f32[8,64,128]{2,1,0:T(8,128)S(1)}, u32[]{:S(2)}, u32[]{:S(2)}) async-start(f32[8,64,128]{2,1,0:T(8,128)} %shard_map.137), calls=%async_computation.5 | async-start | bytes 524288 | tf_op jit(solution)/shard_map/all_to_all | solution.py:432
  111.3 8.8 %collective-permute-start.6 = (f32[80,128]{1,0:T(8,128)S(1)}, f32[80,128]{1,0:T(8,128)S(1)}, u32[]{:S(2)}, u32[]{:S(2)}) collective-permute-start(f32[80,128]{1,0:T(8,128)S(1)} %get-tuple-element.36), channel_id=1, source_target_pairs={{0,1},{1,0},{2,3},{3,2},{4,5},{5,4},{6,7},{7,6},{8,9},{9,8},{10,11... | collective-permute-start | bytes 122888 | tf_op jit(solution)/shard_map/ppermute | solution.py:434
  112.1 12.2 %collective-permute-start.7 = (f32[80,128]{1,0:T(8,128)S(1)}, f32[80,128]{1,0:T(8,128)S(1)}, u32[]{:S(2)}, u32[]{:S(2)}) collective-permute-start(f32[80,128]{1,0:T(8,128)S(1)} %get-tuple-element.37), channel_id=1, source_target_pairs={{1,2},{2,1},{3,4},{4,3},{5,6},{6,5},{9,10},{10,9},{11,12},{12,11},... | collective-permute-start | bytes 122888 | tf_op jit(solution)/shard_map/ppermute | solution.py:433
  138.7 5.7 %collective-permute-start.13 = (f32[6,8,128]{2,1,0:T(8,128)S(1)}, f32[6,8,128]{2,1,0:T(8,128)S(1)}, u32[]{:S(2)}, u32[]{:S(2)}) collective-permute-start(f32[6,8,128]{2,1,0:T(8,128)S(1)} %get-tuple-element.46), channel_id=1, source_target_pairs={{64,128},{128,64},{65,129},{129,65},{66,130},{130,66},{67,131},{13... | collective-permute-start | bytes 73736 | tf_op jit(solution)/shard_map/ppermute | solution.py:425
  141.7 3.9 %collective-permute-start.12 = (f32[6,8,128]{2,1,0:T(8,128)S(1)}, f32[6,8,128]{2,1,0:T(8,128)S(1)}, u32[]{:S(2)}, u32[]{:S(2)}) collective-permute-start(f32[6,8,128]{2,1,0:T(8,128)S(1)} %get-tuple-element.46), channel_id=1, source_target_pairs={{0,64},{64,0},{128,192},{192,128},{1,65},{65,1},{129,193},{193,129... | collective-permute-start | bytes 73736 | tf_op jit(solution)/shard_map/ppermute | solution.py:424
  146.9 24.0 %all-to-all-start.7 = ((f32[8,64,128]{2,1,0:T(8,128)}), f32[8,64,128]{2,1,0:T(8,128)S(1)}, u32[]{:S(2)}, u32[]{:S(2)}) async-start(f32[8,64,128]{2,1,0:T(8,128)} %shard_map.141), calls=%async_computation.7 | async-start | bytes 524288 | tf_op jit(solution)/shard_map/all_to_all | solution.py:432
  154.7 8.7 %collective-permute-start.10 = (f32[80,128]{1,0:T(8,128)S(1)}, f32[80,128]{1,0:T(8,128)S(1)}, u32[]{:S(2)}, u32[]{:S(2)}) collective-permute-start(f32[80,128]{1,0:T(8,128)S(1)} %get-tuple-element.42), channel_id=1, source_target_pairs={{0,1},{1,0},{2,3},{3,2},{4,5},{5,4},{6,7},{7,6},{8,9},{9,8},{10,11... | collective-permute-start | bytes 122888 | tf_op jit(solution)/shard_map/ppermute | solution.py:434
  155.6 12.2 %collective-permute-start.11 = (f32[80,128]{1,0:T(8,128)S(1)}, f32[80,128]{1,0:T(8,128)S(1)}, u32[]{:S(2)}, u32[]{:S(2)}) collective-permute-start(f32[80,128]{1,0:T(8,128)S(1)} %get-tuple-element.43), channel_id=1, source_target_pairs={{1,2},{2,1},{3,4},{4,3},{5,6},{6,5},{9,10},{10,9},{11,12},{12,11},... | collective-permute-start | bytes 122888 | tf_op jit(solution)/shard_map/ppermute | solution.py:433
  172.5 12.7 %all-to-all-start.8 = ((f32[8,56,128]{2,1,0:T(8,128)}), f32[8,56,128]{2,1,0:T(8,128)S(1)}, u32[]{:S(2)}, u32[]{:S(2)}) async-start(f32[8,56,128]{2,1,0:T(8,128)} %shard_map.142), calls=%async_computation.8 | async-start | bytes 458752 | tf_op jit(solution)/shard_map/all_to_all | solution.py:444
  177.3 9.3 %collective-permute-start.14 = (f32[80,128]{1,0:T(8,128)S(1)}, f32[80,128]{1,0:T(8,128)S(1)}, u32[]{:S(2)}, u32[]{:S(2)}) collective-permute-start(f32[80,128]{1,0:T(8,128)S(1)} %get-tuple-element.48), channel_id=1, source_target_pairs={{0,1},{1,0},{2,3},{3,2},{4,5},{5,4},{6,7},{7,6},{8,9},{9,8},{10,11... | collective-permute-start | bytes 122888 | tf_op jit(solution)/shard_map/ppermute | solution.py:434
  177.3 12.0 %collective-permute-start.15 = (f32[80,128]{1,0:T(8,128)S(1)}, f32[80,128]{1,0:T(8,128)S(1)}, u32[]{:S(2)}, u32[]{:S(2)}) collective-permute-start(f32[80,128]{1,0:T(8,128)S(1)} %get-tuple-element.49), channel_id=1, source_target_pairs={{1,2},{2,1},{3,4},{4,3},{5,6},{6,5},{9,10},{10,9},{11,12},{12,11},... | collective-permute-start | bytes 122888 | tf_op jit(solution)/shard_map/ppermute | solution.py:433
  (13 other events, 123.9 us)
where the time goes:
time: 193 us; the launch traced here: 192 us
  starting transfers between devices  85.2 us (44%)
  waiting for transfers between devices  51.2 us (27%)
  Pallas kernels  33.9 us (18%)
  blocking collectives  19.9 us (10%)
    pallas_call x18, Pallas kernels, call(): pl.pallas_call(kernel, out_shape=[jax.ShapeDtypeStruct(o, jnp.float32) fo...  31.7 us
    all_to_all x4, starting transfers between devices, body(): got = lax.all_to_all(send, 'rad', 0, 0)  27.7 us
    ppermute x4, starting transfers between devices, body(): high = lax.ppermute(second_swap, 'rad', swaps(rad_size, 1))  27.7 us
    all_to_all x2, blocking collectives, body(): across = lax.all_to_all(send, 'row', 0, 0)  19.9 us
    ppermute x4, waiting for transfers between devices, body(): high = lax.ppermute(second_swap, 'rad', swaps(rad_size, 1))  19.3 us
    all_to_all x4, waiting for transfers between devices, body(): got = lax.all_to_all(send, 'rad', 0, 0)  16.4 us
    ppermute x4, starting transfers between devices, body(): other_way = lax.ppermute(beside, 'sec', swaps(sections, 1))  12.6 us
    ppermute x4, waiting for transfers between devices, body(): other_way = lax.ppermute(beside, 'sec', swaps(sections, 1))  10 us
  transfers between devices with their start and end apart: 23, of which 14 were waited for; matrix products, arithmetic and copies ran while one was open for 0% of the time, Pallas kernels for 8%

commit v1 on v0

--- a/solution.py
+++ b/solution.py
@@ -132,7 +132,7 @@
         return last, first
 
     zero = jnp.zeros((8, 128), jnp.float32)
-    last, first = lax.fori_loop(0, PLANES, one, (zero, zero))
+    last, first = lax.fori_loop(0, PLANES, one, (zero, zero), unroll=2)
     send[lax.rem(row + 1, size), 8:16, :] = last
     send[lax.rem(row + size - 1, size), 8:16, :] = first
 
@@ -245,7 +245,7 @@
         coef[12, k] = 1.0 - total
         return carry
 
-    lax.fori_loop(0, PLANES, one, 0)
+    lax.fori_loop(0, PLANES, one, 0, unroll=2)
 
 
 def advance(k, before, here, after, coef, matrix, left, right, low, high):
@@ -355,7 +355,7 @@
     last, first = note(0, [ends[0, v] for v in range(NV)], zero, zero)
     last, first = note(PLANES - 1, [ends[1, v] for v in range(NV)], last, first)
     carry = ([field[v, 0] for v in range(NV)], [field[v, 1] for v in range(NV)], last, first)
-    _, _, last, first = lax.fori_loop(1, PLANES - 1, one, carry)
+    _, _, last, first = lax.fori_loop(1, PLANES - 1, one, carry, unroll=2)
     if len(refs) > 2:
         edges[0] = last
         edges[1] = first

time: 193 us -> 190 us (0.984)
  Pallas kernels: 33.9 us -> 29.1 us
    pallas_call x18, Pallas kernels: 31.7 us -> 27 us  [call(): pl.pallas_call(kernel, out_shape=[jax.ShapeDtypeStruct(o, jnp.float32) fo...]
  transfers between devices with their start and end apart: 23 -> 23, of which waited for: 14 -> 14; matrix products, arithmetic and copies ran while one was open for 0% -> 0% of each run, Pallas kernels for 8% -> 6%
where the time goes in v1:
time: 190 us; the launch traced here: 188 us
  starting transfers between devices  85.2 us (45%)
  waiting for transfers between devices  52.3 us (28%)
  Pallas kernels  29.1 us (15%)
  blocking collectives  19.9 us (10%)
    all_to_all x4, starting transfers between devices, body(): got = lax.all_to_all(send, 'rad', 0, 0)  27.7 us
    ppermute x4, starting transfers between devices, body(): high = lax.ppermute(second_swap, 'rad', swaps(rad_size, 1))  27.7 us
    pallas_call x18, Pallas kernels, call(): pl.pallas_call(kernel, out_shape=[jax.ShapeDtypeStruct(o, jnp.float32) fo...  27 us
    all_to_all x2, blocking collectives, body(): across = lax.all_to_all(send, 'row', 0, 0)  19.9 us
    ppermute x4, waiting for transfers between devices, body(): high = lax.ppermute(second_swap, 'rad', swaps(rad_size, 1))  19.3 us
    all_to_all x4, waiting for transfers between devices, body(): got = lax.all_to_all(send, 'rad', 0, 0)  17.5 us
    ppermute x4, starting transfers between devices, body(): other_way = lax.ppermute(beside, 'sec', swaps(sections, 1))  12.6 us
    ppermute x4, waiting for transfers between devices, body(): other_way = lax.ppermute(beside, 'sec', swaps(sections, 1))  10 us
  transfers between devices with their start and end apart: 23, of which 14 were waited for; matrix products, arithmetic and copies ran while one was open for 0% of the time, Pallas kernels for 6%

profile of v1, /device:TPU:46, one launch (start us, length us, event | category | flops | bytes accessed | tf_op | source)
XLA Modules:
  0.0 188.3 jit_solution(14405157086016746169)
XLA Ops:
  0.7 3.4 %shard_map.127 = (f32[8,128]{1,0:T(8,128)}, f32[8,16,128]{2,1,0:T(8,128)}, f32[112,128]{1,0:T(8,128)}, f32[112,128]{1,0:T(8,128)}) custom-call(s32[6]{0:T(128)} %stack.15.ids, f32[5]{0:T(128)} %weight.11, s32[8]{0:T(128)} %bitcast.35, s32[8]{0:T(128)} %bitcast.36, f32[5,16,8,128]{3,2,1,0:T(8,128)} %bitcast.15, f32[16,8,128]{2,1,0:T(8,128)} %bitcast.27, ...), custom_call_target="tpu_custom_call" | custom-call | bytes 184320 | tf_op jit(solution)/shard_map/pallas_call | solution.py:41
  4.1 4.9 %all-to-all-start = ((f32[8,16,128]{2,1,0:T(8,128)}), f32[8,16,128]{2,1,0:T(8,128)S(1)}, u32[]{:S(2)}, u32[]{:S(2)}) async-start(f32[8,16,128]{2,1,0:T(8,128)} %get-tuple-element.28), calls=%async_computation | async-start | bytes 131072 | tf_op jit(solution)/shard_map/all_to_all | solution.py:418
  11.2 3.8 %collective-permute-start.3 = (f32[6,8,128]{2,1,0:T(8,128)}, f32[6,8,128]{2,1,0:T(8,128)S(1)}, u32[]{:S(2)}, u32[]{:S(2)}) collective-permute-start(f32[6,8,128]{2,1,0:T(8,128)} %beside.1), channel_id=1, source_target_pairs={{64,128},{128,64},{65,129},{129,65},{66,130},{130,66},{67,131},{13... | collective-permute-start | bytes 73736 | tf_op jit(solution)/shard_map/ppermute | solution.py:425
  20.4 9.6 %all-to-all-start.1 = ((f32[8,48,128]{2,1,0:T(8,128)}), f32[8,48,128]{2,1,0:T(8,128)S(1)}, u32[]{:S(2)}, u32[]{:S(2)}) async-start(f32[8,48,128]{2,1,0:T(8,128)} %shard_map.129), calls=%async_computation.1 | async-start | bytes 393216 | tf_op jit(solution)/shard_map/all_to_all | solution.py:432
  30.0 9.5 %all-to-all-done.1.got = f32[8,48,128]{2,1,0:T(8,128)S(1)} async-done(((f32[8,48,128]{2,1,0:T(8,128)}), f32[8,48,128]{2,1,0:T(8,128)S(1)}, u32[]{:S(2)}, u32[]{:S(2)}) %all-to-all-start.1) | async-done | bytes 196640 | tf_op jit(solution)/shard_map/all_to_all | solution.py:432
  41.2 4.9 %all-to-all-start.2 = ((f32[8,48,128]{2,1,0:T(8,128)}), f32[8,48,128]{2,1,0:T(8,128)S(1)}, u32[]{:S(2)}, u32[]{:S(2)}) async-start(f32[8,48,128]{2,1,0:T(8,128)} %shard_map.130), calls=%async_computation.2 | async-start | bytes 393216 | tf_op jit(solution)/shard_map/all_to_all | solution.py:444
  46.6 4.0 %collective-permute-start.1 = (f32[112,128]{1,0:T(8,128)S(1)}, f32[112,128]{1,0:T(8,128)S(1)}, u32[]{:S(2)}, u32[]{:S(2)}) collective-permute-start(f32[112,128]{1,0:T(8,128)S(1)} %copy-done.12), channel_id=1, source_target_pairs={{1,2},{2,1},{3,4},{4,3},{5,6},{6,5},{9,10},{10,9},{11,12},{12,11},... | collective-permute-start | bytes 172040 | tf_op jit(solution)/shard_map/ppermute | solution.py:433
  50.8 8.0 %collective-permute-done.1.second_swap.refs_1_.from_second = f32[112,128]{1,0:T(8,128)S(1)} collective-permute-done((f32[112,128]{1,0:T(8,128)S(1)}, f32[112,128]{1,0:T(8,128)S(1)}, u32[]{:S(2)}, u32[]{:S(2)}) %collective-permute-start.1) | collective-permute-done | bytes 57376 | tf_op jit(solution)/shard_map/ppermute | solution.py:433
  61.6 2.9 %collective-permute-start.5 = (f32[6,8,128]{2,1,0:T(8,128)S(1)}, f32[6,8,128]{2,1,0:T(8,128)S(1)}, u32[]{:S(2)}, u32[]{:S(2)}) collective-permute-start(f32[6,8,128]{2,1,0:T(8,128)S(1)} %get-tuple-element.34), channel_id=1, source_target_pairs={{64,128},{128,64},{65,129},{129,65},{66,130},{130,66},{67,131},{13... | collective-permute-start | bytes 73736 | tf_op jit(solution)/shard_map/ppermute | solution.py:425
  69.7 4.5 %all-to-all-start.3 = ((f32[8,64,128]{2,1,0:T(8,128)}), f32[8,64,128]{2,1,0:T(8,128)S(1)}, u32[]{:S(2)}, u32[]{:S(2)}) async-start(f32[8,64,128]{2,1,0:T(8,128)} %shard_map.133), calls=%async_computation.3 | async-start | bytes 524288 | tf_op jit(solution)/shard_map/all_to_all | solution.py:432
  76.3 8.0 %all-to-all-done.3.got.refs_0_ = f32[8,64,128]{2,1,0:T(8,128)S(1)} async-done(((f32[8,64,128]{2,1,0:T(8,128)}), f32[8,64,128]{2,1,0:T(8,128)S(1)}, u32[]{:S(2)}, u32[]{:S(2)}) %all-to-all-start.3) | async-done | bytes 262176 | tf_op jit(solution)/shard_map/all_to_all | solution.py:432
  85.2 10.3 %all_to_all.45.across.around = f32[8,56,128]{2,1,0:T(8,128)S(1)} all-to-all(f32[8,56,128]{2,1,0:T(8,128)S(1)} %shard_map.134), channel_id=1, replica_groups=mesh['sec'=4,'row'=8,'rad'=8] {'row'}, dimensions={0} | all-to-all | bytes 458752 | tf_op jit(solution)/shard_map/all_to_all | solution.py:444
  96.3 2.9 %collective-permute-start.9 = (f32[6,8,128]{2,1,0:T(8,128)S(1)}, f32[6,8,128]{2,1,0:T(8,128)S(1)}, u32[]{:S(2)}, u32[]{:S(2)}) collective-permute-start(f32[6,8,128]{2,1,0:T(8,128)S(1)} %get-tuple-element.40), channel_id=1, source_target_pairs={{64,128},{128,64},{65,129},{129,65},{66,130},{130,66},{67,131},{13... | collective-permute-start | bytes 73736 | tf_op jit(solution)/shard_map/ppermute | solution.py:425
  104.4 5.7 %all-to-all-start.5 = ((f32[8,64,128]{2,1,0:T(8,128)}), f32[8,64,128]{2,1,0:T(8,128)S(1)}, u32[]{:S(2)}, u32[]{:S(2)}) async-start(f32[8,64,128]{2,1,0:T(8,128)} %shard_map.137), calls=%async_computation.5 | async-start | bytes 524288 | tf_op jit(solution)/shard_map/all_to_all | solution.py:432
  111.0 7.9 %collective-permute-start.7 = (f32[80,128]{1,0:T(8,128)S(1)}, f32[80,128]{1,0:T(8,128)S(1)}, u32[]{:S(2)}, u32[]{:S(2)}) collective-permute-start(f32[80,128]{1,0:T(8,128)S(1)} %get-tuple-element.37), channel_id=1, source_target_pairs={{1,2},{2,1},{3,4},{4,3},{5,6},{6,5},{9,10},{10,9},{11,12},{12,11},... | collective-permute-start | bytes 122888 | tf_op jit(solution)/shard_map/ppermute | solution.py:433
  118.9 4.3 %collective-permute-done.7.from_second = f32[80,128]{1,0:T(8,128)S(1)} collective-permute-done((f32[80,128]{1,0:T(8,128)S(1)}, f32[80,128]{1,0:T(8,128)S(1)}, u32[]{:S(2)}, u32[]{:S(2)}) %collective-permute-start.7) | collective-permute-done | bytes 40992 | tf_op jit(solution)/shard_map/ppermute | solution.py:433
  126.3 9.6 %all_to_all.46.across.around = f32[8,56,128]{2,1,0:T(8,128)S(1)} all-to-all(f32[8,56,128]{2,1,0:T(8,128)S(1)} %shard_map.138), channel_id=1, replica_groups=mesh['sec'=4,'row'=8,'rad'=8] {'row'}, dimensions={0} | all-to-all | bytes 458752 | tf_op jit(solution)/shard_map/all_to_all | solution.py:444
  136.6 2.9 %collective-permute-start.13 = (f32[6,8,128]{2,1,0:T(8,128)S(1)}, f32[6,8,128]{2,1,0:T(8,128)S(1)}, u32[]{:S(2)}, u32[]{:S(2)}) collective-permute-start(f32[6,8,128]{2,1,0:T(8,128)S(1)} %get-tuple-element.46), channel_id=1, source_target_pairs={{64,128},{128,64},{65,129},{129,65},{66,130},{130,66},{67,131},{13... | collective-permute-start | bytes 73736 | tf_op jit(solution)/shard_map/ppermute | solution.py:425
  144.7 7.8 %all-to-all-start.7 = ((f32[8,64,128]{2,1,0:T(8,128)}), f32[8,64,128]{2,1,0:T(8,128)S(1)}, u32[]{:S(2)}, u32[]{:S(2)}) async-start(f32[8,64,128]{2,1,0:T(8,128)} %shard_map.141), calls=%async_computation.7 | async-start | bytes 524288 | tf_op jit(solution)/shard_map/all_to_all | solution.py:432
  153.4 7.9 %collective-permute-start.11 = (f32[80,128]{1,0:T(8,128)S(1)}, f32[80,128]{1,0:T(8,128)S(1)}, u32[]{:S(2)}, u32[]{:S(2)}) collective-permute-start(f32[80,128]{1,0:T(8,128)S(1)} %get-tuple-element.43), channel_id=1, source_target_pairs={{1,2},{2,1},{3,4},{4,3},{5,6},{6,5},{9,10},{10,9},{11,12},{12,11},... | collective-permute-start | bytes 122888 | tf_op jit(solution)/shard_map/ppermute | solution.py:433
  161.3 4.3 %collective-permute-done.11.from_second = f32[80,128]{1,0:T(8,128)S(1)} collective-permute-done((f32[80,128]{1,0:T(8,128)S(1)}, f32[80,128]{1,0:T(8,128)S(1)}, u32[]{:S(2)}, u32[]{:S(2)}) %collective-permute-start.11) | collective-permute-done | bytes 40992 | tf_op jit(solution)/shard_map/ppermute | solution.py:433
  169.4 4.8 %all-to-all-start.8 = ((f32[8,56,128]{2,1,0:T(8,128)}), f32[8,56,128]{2,1,0:T(8,128)S(1)}, u32[]{:S(2)}, u32[]{:S(2)}) async-start(f32[8,56,128]{2,1,0:T(8,128)} %shard_map.142), calls=%async_computation.8 | async-start | bytes 458752 | tf_op jit(solution)/shard_map/all_to_all | solution.py:444
  174.1 7.9 %collective-permute-start.15 = (f32[80,128]{1,0:T(8,128)S(1)}, f32[80,128]{1,0:T(8,128)S(1)}, u32[]{:S(2)}, u32[]{:S(2)}) collective-permute-start(f32[80,128]{1,0:T(8,128)S(1)} %get-tuple-element.49), channel_id=1, source_target_pairs={{1,2},{2,1},{3,4},{4,3},{5,6},{6,5},{9,10},{10,9},{11,12},{12,11},... | collective-permute-start | bytes 122888 | tf_op jit(solution)/shard_map/ppermute | solution.py:433
  183.4 2.7 %collective-permute-done.15.from_second = f32[80,128]{1,0:T(8,128)S(1)} collective-permute-done((f32[80,128]{1,0:T(8,128)S(1)}, f32[80,128]{1,0:T(8,128)S(1)}, u32[]{:S(2)}, u32[]{:S(2)}) %collective-permute-start.15) | collective-permute-done | bytes 40992 | tf_op jit(solution)/shard_map/ppermute | solution.py:433
  (77 shorter events, 45.3 us)
Async XLA Ops:
  4.1 16.3 %all-to-all-start = ((f32[8,16,128]{2,1,0:T(8,128)}), f32[8,16,128]{2,1,0:T(8,128)S(1)}, u32[]{:S(2)}, u32[]{:S(2)}) async-start(f32[8,16,128]{2,1,0:T(8,128)} %get-tuple-element.28), calls=%async_computation | async-start | bytes 131072 | tf_op jit(solution)/shard_map/all_to_all | solution.py:418
  11.2 5.9 %collective-permute-start.3 = (f32[6,8,128]{2,1,0:T(8,128)}, f32[6,8,128]{2,1,0:T(8,128)S(1)}, u32[]{:S(2)}, u32[]{:S(2)}) collective-permute-start(f32[6,8,128]{2,1,0:T(8,128)} %beside.1), channel_id=1, source_target_pairs={{64,128},{128,64},{65,129},{129,65},{66,130},{130,66},{67,131},{13... | collective-permute-start | bytes 73736 | tf_op jit(solution)/shard_map/ppermute | solution.py:425
  15.0 4.1 %collective-permute-start.2 = (f32[6,8,128]{2,1,0:T(8,128)}, f32[6,8,128]{2,1,0:T(8,128)S(1)}, u32[]{:S(2)}, u32[]{:S(2)}) collective-permute-start(f32[6,8,128]{2,1,0:T(8,128)} %beside.1), channel_id=1, source_target_pairs={{0,64},{64,0},{128,192},{192,128},{1,65},{65,1},{129,193},{193,129... | collective-permute-start | bytes 73736 | tf_op jit(solution)/shard_map/ppermute | solution.py:424
  20.4 19.1 %all-to-all-start.1 = ((f32[8,48,128]{2,1,0:T(8,128)}), f32[8,48,128]{2,1,0:T(8,128)S(1)}, u32[]{:S(2)}, u32[]{:S(2)}) async-start(f32[8,48,128]{2,1,0:T(8,128)} %shard_map.129), calls=%async_computation.1 | async-start | bytes 393216 | tf_op jit(solution)/shard_map/all_to_all | solution.py:432
  41.1 17.7 %copy-start.3 = (f32[1,16,8,128]{3,2,1,0:T(8,128)S(1)}, f32[1,16,8,128]{3,2,1,0:T(8,128)}, u32[]{:S(2)}) copy-start(f32[1,16,8,128]{3,2,1,0:T(8,128)} %param.17) | copy-start | bytes 196612
  41.2 19.0 %all-to-all-start.2 = ((f32[8,48,128]{2,1,0:T(8,128)}), f32[8,48,128]{2,1,0:T(8,128)S(1)}, u32[]{:S(2)}, u32[]{:S(2)}) async-start(f32[8,48,128]{2,1,0:T(8,128)} %shard_map.130), calls=%async_computation.2 | async-start | bytes 393216 | tf_op jit(solution)/shard_map/all_to_all | solution.py:444
  46.1 4.7 %collective-permute-start = (f32[112,128]{1,0:T(8,128)S(1)}, f32[112,128]{1,0:T(8,128)S(1)}, u32[]{:S(2)}, u32[]{:S(2)}) collective-permute-start(f32[112,128]{1,0:T(8,128)S(1)} %copy-done.13), channel_id=1, source_target_pairs={{0,1},{1,0},{2,3},{3,2},{4,5},{5,4},{6,7},{7,6},{8,9},{9,8},{10,11... | collective-permute-start | bytes 172040 | tf_op jit(solution)/shard_map/ppermute | solution.py:434
  46.6 12.2 %collective-permute-start.1 = (f32[112,128]{1,0:T(8,128)S(1)}, f32[112,128]{1,0:T(8,128)S(1)}, u32[]{:S(2)}, u32[]{:S(2)}) collective-permute-start(f32[112,128]{1,0:T(8,128)S(1)} %copy-done.12), channel_id=1, source_target_pairs={{1,2},{2,1},{3,4},{4,3},{5,6},{6,5},{9,10},{10,9},{11,12},{12,11},... | collective-permute-start | bytes 172040 | tf_op jit(solution)/shard_map/ppermute | solution.py:433
  61.6 5.7 %collective-permute-start.5 = (f32[6,8,128]{2,1,0:T(8,128)S(1)}, f32[6,8,128]{2,1,0:T(8,128)S(1)}, u32[]{:S(2)}, u32[]{:S(2)}) collective-permute-start(f32[6,8,128]{2,1,0:T(8,128)S(1)} %get-tuple-element.34), channel_id=1, source_target_pairs={{64,128},{128,64},{65,129},{129,65},{66,130},{130,66},{67,131},{13... | collective-permute-start | bytes 73736 | tf_op jit(solution)/shard_map/ppermute | solution.py:425
  64.5 3.9 %collective-permute-start.4 = (f32[6,8,128]{2,1,0:T(8,128)S(1)}, f32[6,8,128]{2,1,0:T(8,128)S(1)}, u32[]{:S(2)}, u32[]{:S(2)}) collective-permute-start(f32[6,8,128]{2,1,0:T(8,128)S(1)} %get-tuple-element.34), channel_id=1, source_target_pairs={{0,64},{64,0},{128,192},{192,128},{1,65},{65,1},{129,193},{193,129... | collective-permute-start | bytes 73736 | tf_op jit(solution)/shard_map/ppermute | solution.py:424
  69.7 14.5 %all-to-all-start.3 = ((f32[8,64,128]{2,1,0:T(8,128)}), f32[8,64,128]{2,1,0:T(8,128)S(1)}, u32[]{:S(2)}, u32[]{:S(2)}) async-start(f32[8,64,128]{2,1,0:T(8,128)} %shard_map.133), calls=%async_computation.3 | async-start | bytes 524288 | tf_op jit(solution)/shard_map/all_to_all | solution.py:432
  96.3 5.7 %collective-permute-start.9 = (f32[6,8,128]{2,1,0:T(8,128)S(1)}, f32[6,8,128]{2,1,0:T(8,128)S(1)}, u32[]{:S(2)}, u32[]{:S(2)}) collective-permute-start(f32[6,8,128]{2,1,0:T(8,128)S(1)} %get-tuple-element.40), channel_id=1, source_target_pairs={{64,128},{128,64},{65,129},{129,65},{66,130},{130,66},{67,131},{13... | collective-permute-start | bytes 73736 | tf_op jit(solution)/shard_map/ppermute | solution.py:425
  99.2 3.9 %collective-permute-start.8 = (f32[6,8,128]{2,1,0:T(8,128)S(1)}, f32[6,8,128]{2,1,0:T(8,128)S(1)}, u32[]{:S(2)}, u32[]{:S(2)}) collective-permute-start(f32[6,8,128]{2,1,0:T(8,128)S(1)} %get-tuple-element.40), channel_id=1, source_target_pairs={{0,64},{64,0},{128,192},{192,128},{1,65},{65,1},{129,193},{193,129... | collective-permute-start | bytes 73736 | tf_op jit(solution)/shard_map/ppermute | solution.py:424
  104.4 20.9 %all-to-all-start.5 = ((f32[8,64,128]{2,1,0:T(8,128)}), f32[8,64,128]{2,1,0:T(8,128)S(1)}, u32[]{:S(2)}, u32[]{:S(2)}) async-start(f32[8,64,128]{2,1,0:T(8,128)} %shard_map.137), calls=%async_computation.5 | async-start | bytes 524288 | tf_op jit(solution)/shard_map/all_to_all | solution.py:432
  110.2 8.8 %collective-permute-start.6 = (f32[80,128]{1,0:T(8,128)S(1)}, f32[80,128]{1,0:T(8,128)S(1)}, u32[]{:S(2)}, u32[]{:S(2)}) collective-permute-start(f32[80,128]{1,0:T(8,128)S(1)} %get-tuple-element.36), channel_id=1, source_target_pairs={{0,1},{1,0},{2,3},{3,2},{4,5},{5,4},{6,7},{7,6},{8,9},{9,8},{10,11... | collective-permute-start | bytes 122888 | tf_op jit(solution)/shard_map/ppermute | solution.py:434
  111.0 12.2 %collective-permute-start.7 = (f32[80,128]{1,0:T(8,128)S(1)}, f32[80,128]{1,0:T(8,128)S(1)}, u32[]{:S(2)}, u32[]{:S(2)}) collective-permute-start(f32[80,128]{1,0:T(8,128)S(1)} %get-tuple-element.37), channel_id=1, source_target_pairs={{1,2},{2,1},{3,4},{4,3},{5,6},{6,5},{9,10},{10,9},{11,12},{12,11},... | collective-permute-start | bytes 122888 | tf_op jit(solution)/shard_map/ppermute | solution.py:433
  136.6 5.7 %collective-permute-start.13 = (f32[6,8,128]{2,1,0:T(8,128)S(1)}, f32[6,8,128]{2,1,0:T(8,128)S(1)}, u32[]{:S(2)}, u32[]{:S(2)}) collective-permute-start(f32[6,8,128]{2,1,0:T(8,128)S(1)} %get-tuple-element.46), channel_id=1, source_target_pairs={{64,128},{128,64},{65,129},{129,65},{66,130},{130,66},{67,131},{13... | collective-permute-start | bytes 73736 | tf_op jit(solution)/shard_map/ppermute | solution.py:425
  139.5 3.9 %collective-permute-start.12 = (f32[6,8,128]{2,1,0:T(8,128)S(1)}, f32[6,8,128]{2,1,0:T(8,128)S(1)}, u32[]{:S(2)}, u32[]{:S(2)}) collective-permute-start(f32[6,8,128]{2,1,0:T(8,128)S(1)} %get-tuple-element.46), channel_id=1, source_target_pairs={{0,64},{64,0},{128,192},{192,128},{1,65},{65,1},{129,193},{193,129... | collective-permute-start | bytes 73736 | tf_op jit(solution)/shard_map/ppermute | solution.py:424
  144.7 22.9 %all-to-all-start.7 = ((f32[8,64,128]{2,1,0:T(8,128)}), f32[8,64,128]{2,1,0:T(8,128)S(1)}, u32[]{:S(2)}, u32[]{:S(2)}) async-start(f32[8,64,128]{2,1,0:T(8,128)} %shard_map.141), calls=%async_computation.7 | async-start | bytes 524288 | tf_op jit(solution)/shard_map/all_to_all | solution.py:432
  152.6 8.7 %collective-permute-start.10 = (f32[80,128]{1,0:T(8,128)S(1)}, f32[80,128]{1,0:T(8,128)S(1)}, u32[]{:S(2)}, u32[]{:S(2)}) collective-permute-start(f32[80,128]{1,0:T(8,128)S(1)} %get-tuple-element.42), channel_id=1, source_target_pairs={{0,1},{1,0},{2,3},{3,2},{4,5},{5,4},{6,7},{7,6},{8,9},{9,8},{10,11... | collective-permute-start | bytes 122888 | tf_op jit(solution)/shard_map/ppermute | solution.py:434
  153.4 12.2 %collective-permute-start.11 = (f32[80,128]{1,0:T(8,128)S(1)}, f32[80,128]{1,0:T(8,128)S(1)}, u32[]{:S(2)}, u32[]{:S(2)}) collective-permute-start(f32[80,128]{1,0:T(8,128)S(1)} %get-tuple-element.43), channel_id=1, source_target_pairs={{1,2},{2,1},{3,4},{4,3},{5,6},{6,5},{9,10},{10,9},{11,12},{12,11},... | collective-permute-start | bytes 122888 | tf_op jit(solution)/shard_map/ppermute | solution.py:433
  169.4 12.7 %all-to-all-start.8 = ((f32[8,56,128]{2,1,0:T(8,128)}), f32[8,56,128]{2,1,0:T(8,128)S(1)}, u32[]{:S(2)}, u32[]{:S(2)}) async-start(f32[8,56,128]{2,1,0:T(8,128)} %shard_map.142), calls=%async_computation.8 | async-start | bytes 458752 | tf_op jit(solution)/shard_map/all_to_all | solution.py:444
  174.1 9.3 %collective-permute-start.14 = (f32[80,128]{1,0:T(8,128)S(1)}, f32[80,128]{1,0:T(8,128)S(1)}, u32[]{:S(2)}, u32[]{:S(2)}) collective-permute-start(f32[80,128]{1,0:T(8,128)S(1)} %get-tuple-element.48), channel_id=1, source_target_pairs={{0,1},{1,0},{2,3},{3,2},{4,5},{5,4},{6,7},{7,6},{8,9},{9,8},{10,11... | collective-permute-start | bytes 122888 | tf_op jit(solution)/shard_map/ppermute | solution.py:434
  174.1 12.0 %collective-permute-start.15 = (f32[80,128]{1,0:T(8,128)S(1)}, f32[80,128]{1,0:T(8,128)S(1)}, u32[]{:S(2)}, u32[]{:S(2)}) collective-permute-start(f32[80,128]{1,0:T(8,128)S(1)} %get-tuple-element.49), channel_id=1, source_target_pairs={{1,2},{2,1},{3,4},{4,3},{5,6},{6,5},{9,10},{10,9},{11,12},{12,11},... | collective-permute-start | bytes 122888 | tf_op jit(solution)/shard_map/ppermute | solution.py:433
  (13 other events, 123.4 us)
